TPU v7x, 128 devices: a whole 4x4x4 slice. The times are simulated.
128 devices in a mesh: ent: 32 (over x, z, y_lo), qry: 4 (over y_hi, core).
Axes of the slice: x: 4, y: 4 (y_hi: 2, y_lo: 2; y = y_hi * 2 + y_lo), z: 4, core: 2. Of those that a mesh axis runs over, the one named last changes fastest.
Arguments:
- ent_emb: bfloat16 [65536, 512], P('ent'), may hold values from -1 to 1
- ent_tan: bfloat16 [65536, 512], P('ent'), may hold values from -0.25 to 0.25
- qry_emb: bfloat16 [4096, 512], P(('qry', 'ent')), may hold values from -6 to 6
- qry_tan: bfloat16 [4096, 512], P(('qry', 'ent')), may hold values from -6 to 6
- tails: int32 [4096, 4], P('qry'), may hold values from 0 to 65535
Outputs:
- ent_gnvp: float32 [65536, 512], P(('ent', 'qry'))
- ent_grad: float32 [65536, 512], P(('ent', 'qry'))
- qry_gnvp: float32 [4096, 512], P(('qry', 'ent'))
- qry_grad: float32 [4096, 512], P(('qry', 'ent'))
All inputs are finite; a program needn't handle non-finite values.
Results may differ from a plain program's by a relative error of at most 0.0008.
Values may be sent and summed in bfloat16 or wider, within the bound.
A program may use at most 128 MiB of HBM per device.

v0:
```python
import jax
import jax.numpy as jnp
from jax import lax
from jax.sharding import PartitionSpec as P


def dot_nt(a, b):
    return lax.dot_general(a, b, (((1,), (1,)), ((), ())), preferred_element_type=jnp.float32)


def dot_tn(a, b):
    return lax.dot_general(a, b, (((0,), (0,)), ((), ())), preferred_element_type=jnp.float32)


def weights(queries, qtangent, tail_rows, entities, etangent, ent_ids):
    score = dot_nt(queries, entities)
    dscore = dot_nt(qtangent, entities) + dot_nt(queries, etangent)
    prob = jax.nn.sigmoid(score)
    label = jnp.zeros(score.shape, jnp.float32)
    for k in range(tail_rows.shape[1]):
        label = jnp.maximum(
            label, (tail_rows[:, k : k + 1] == ent_ids[None, :]).astype(jnp.float32)
        )
    ugrad = (prob - label).astype(jnp.bfloat16)
    uhess = (prob * (1.0 - prob) * dscore).astype(jnp.bfloat16)
    return (uhess, ugrad)


def per_device(ent_emb, ent_tan, qry_emb, qry_tan, tails):
    ent_rows = ent_emb.shape[0]
    width = ent_emb.shape[1]
    panel_q, panel_dq = (
        lax.all_gather(qry_emb, "ent", axis=0, tiled=True),
        lax.all_gather(qry_tan, "ent", axis=0, tiled=True),
    )
    entities, etangent = (ent_emb, ent_tan)
    ent_ids = lax.axis_index("ent") * ent_rows + jnp.arange(ent_rows, dtype=jnp.int32)
    queries, qtangent, tail_rows = (panel_q, panel_dq, tails)
    uhess, ugrad = weights(queries, qtangent, tail_rows, entities, etangent, ent_ids)
    qrows = lax.psum_scatter(
        jnp.concatenate(
            [
                jnp.dot(uhess, entities, preferred_element_type=jnp.float32),
                jnp.dot(ugrad, entities, preferred_element_type=jnp.float32),
            ],
            axis=1,
        ),
        "ent",
        scatter_dimension=0,
        tiled=True,
    )
    erows = lax.psum_scatter(
        jnp.concatenate([dot_tn(uhess, queries), dot_tn(ugrad, queries)], axis=1),
        "qry",
        scatter_dimension=0,
        tiled=True,
    )
    return (erows[:, :width], erows[:, width:], qrows[:, :width], qrows[:, width:])


def solution(mesh):
    return jax.shard_map(
        per_device,
        mesh=mesh,
        in_specs=(
            P("ent", None),
            P("ent", None),
            P(("qry", "ent"), None),
            P(("qry", "ent"), None),
            P("qry", None),
        ),
        out_specs=(
            P(("ent", "qry"), None),
            P(("ent", "qry"), None),
            P(("qry", "ent"), None),
            P(("qry", "ent"), None),
        ),
        check_vma=False,
    )
```

profile of v0, /device:TPU:0, one launch (start us, length us, event | category | flops | bytes accessed | tf_op | source)
XLA Modules:
  0.0 605.6 jit_solution(13524694855700156160)
XLA Ops:
  7.2 0.0 copy-start
  7.2 0.0 all-gather.5.cloned.1.call-start
  7.2 0.7 all-gather.5.cloned.1.call-update
  7.9 0.0 all-gather.3.cloned.1.call-start
  8.0 0.7 all-gather.3.cloned.1.call-update
  8.7 0.0 reduce-scatter.7.cloned.1.call-start
  8.7 0.9 fusion.4
  9.6 153.4 %all-gather.5.cloned.1.call-done = bf16[1024,512]{1,0:T(8,128)(2,1)} async-done(((bf16[32,512]{1,0:T(8,128)(2,1)}), bf16[1024,512]{1,0:T(8,128)(2,1)}) %all-gather.5.cloned.1.call-update) | async-done | bytes 1048592 | tf_op jit(solution)/shard_map/all_gather | solution.py:34
  163.0 0.0 copy-done
  163.0 6.8 %fusion.5 = f32[1024,2048]{1,0:T(8,128)} fusion(bf16[1024,512]{1,0:T(8,128)(2,1)} %all-gather.5.cloned.1.call-done, bf16[2048,512]{1,0:T(8,128)(2,1)S(1)} %copy-done), kind=kOutput, calls=%fused_computation.11 | convolution fusion | flops 2147483648 | bytes 11534336 | tf_op jit(solution)/shard_map/dot_general | solution.py:8
  169.8 145.9 %all-gather.3.cloned.1.call-done = bf16[1024,512]{1,0:T(8,128)(2,1)} async-done(((bf16[32,512]{1,0:T(8,128)(2,1)}), bf16[1024,512]{1,0:T(8,128)(2,1)}) %all-gather.3.cloned.1.call-update) | async-done | bytes 1048592 | tf_op jit(solution)/shard_map/all_gather | solution.py:33
  315.7 0.0 copy-start.2
  315.7 8.4 %subtract_convert_fusion = (bf16[1024,2048]{1,0:T(8,128)(2,1)}, f32[1024,2048]{1,0:T(8,128)S(1)}) fusion(s32[2048]{0:T(1024)S(1)} %iota_add_fusion, s32[1024]{0:T(1024)S(1)} %bitcast.21, s32[1024]{0:T(1024)S(1)} %bitcast.22, s32[1024]{0:T(1024)S(1)} %bitcast.20, s32[1024]{0:T(1024)S(1)} %bitcast.19, bf16[1024,512]{1,0:T(8,128)(2,1)} %all-gather.3.cloned.1.call-done, ...), kind=kOutput, calls=%fused_computation.4 | convolution fusion | flops 2183135232 | bytes 15753216 | tf_op jit(solution)/shard_map/dot_general | solution.py:8
  324.1 0.0 copy-done.2
  324.1 6.5 %fusion.1 = bf16[1024,2048]{1,0:T(8,128)(2,1)} fusion(f32[1024,2048]{1,0:T(8,128)S(1)} %get-tuple-element.21, f32[1024,2048]{1,0:T(8,128)S(1)} %copy-done.2, bf16[1024,512]{1,0:T(8,128)(2,1)} %all-gather.3.cloned.1.call-done, bf16[2048,512]{1,0:T(8,128)(2,1)} %param.6), kind=kOutput, calls=%fused_computation.2 | convolution fusion | flops 2157969408 | bytes 24117248 | tf_op jit(solution)/shard_map/dot_general | solution.py:8
  330.6 0.0 copy-start.4
  330.6 4.7 fusion.8
  335.3 0.0 copy-done.4
  335.3 2.4 fusion.9
  337.8 2.5 pad_maximum_fusion.1
  340.3 5.4 copy.17
  345.6 0.0 copy-start.3
  345.6 0.0 reduce-scatter.7.cloned.1.call-update
  345.7 0.2 reduce-scatter.5.cloned.1.call-start
  345.9 1.0 copy-done.3
  346.9 0.0 copy-start.5
  346.9 4.7 fusion.6
  351.6 0.0 copy-done.5
  351.6 2.5 fusion.7
  354.1 3.8 pad_maximum_fusion
  357.9 0.0 reduce-scatter.5.cloned.1.call-update
  357.9 158.0 %reduce-scatter.7.cloned.1.call-done = f32[32,1024]{1,0:T(8,128)} async-done(((f32[1024,1024]{1,0:T(8,128)}), f32[32,1024]{1,0:T(8,128)}) %reduce-scatter.7.cloned.1.call-update) | async-done | bytes 131088
  515.9 0.0 copy-start.1
  515.9 1.7 fusion.3
  517.6 75.0 %reduce-scatter.5.cloned.1.call-done = f32[512,1024]{0,1:T(8,128)} async-done(((f32[2048,1024]{0,1:T(8,128)}), f32[512,1024]{0,1:T(8,128)}) %reduce-scatter.5.cloned.1.call-update) | async-done | bytes 2097168 | tf_op jit(solution)/shard_map/reduce_scatter | solution.py:52
  592.6 2.7 fusion.2
  595.3 2.5 copy.14
  597.8 1.3 copy.13
  599.1 0.0 copy-done.1
  (1 shorter events, 0.0 us)
Async XLA Ops:
  7.2 155.8 %copy-start = (bf16[2048,512]{1,0:T(8,128)(2,1)S(1)}, bf16[2048,512]{1,0:T(8,128)(2,1)}, u32[]{:S(2)}) copy-start(bf16[2048,512]{1,0:T(8,128)(2,1)} %param.5) | copy-start | bytes 6291460
  7.2 155.8 %all-gather.5.cloned.1.call-start = ((), (), s32[]{:S(2)}) async-start(), calls=%async_computation.3 | async-start | bytes 1081344 | tf_op jit(solution)/shard_map/all_gather | solution.py:34
  7.9 307.8 %all-gather.3.cloned.1.call-start = ((), (), s32[]{:S(2)}) async-start(), calls=%async_computation.2 | async-start | bytes 1081344 | tf_op jit(solution)/shard_map/all_gather | solution.py:33
  8.7 507.3 %reduce-scatter.7.cloned.1.call-start = ((), (), s32[]{:S(2)}) async-start(), calls=%async_computation.5 | async-start | bytes 4325376
  315.7 8.4 %copy-start.2 = (f32[1024,2048]{1,0:T(8,128)S(1)}, f32[1024,2048]{1,0:T(8,128)}, u32[]{:S(2)}) copy-start(f32[1024,2048]{1,0:T(8,128)} %fusion.5) | copy-start | bytes 25165828
  330.6 4.7 copy-start.4
  345.6 1.2 copy-start.3
  345.7 246.9 %reduce-scatter.5.cloned.1.call-start = ((), (), s32[]{:S(2)}) async-start(), calls=%async_computation.4 | async-start | bytes 10485760 | tf_op jit(solution)/shard_map/reduce_scatter | solution.py:52
  346.9 4.7 copy-start.5
  515.9 83.2 %copy-start.1 = (bf16[2048,512]{1,0:T(8,128)(2,1)S(1)}, bf16[2048,512]{1,0:T(8,128)(2,1)}, u32[]{:S(2)}) copy-start(bf16[2048,512]{1,0:T(8,128)(2,1)} %param.5) | copy-start | bytes 6291460
Sparse Core Ops, SparseCore 0:
  9.7 153.2 all-gather.4
  164.6 151.0 all-gather.2
  345.8 170.1 reduce-scatter.6
  518.5 74.0 reduce-scatter.4
where the time goes:
time: 607 us; the launch traced here: 606 us
  waiting for transfers between devices  534 us (88%)
  matrix products  36.1 us (6%)
  local copies, waits for them, and re-layouts  15.4 us (3%)
  between operations  13.8 us (2%)
  other arithmetic  6.33 us (1%)
    unnamed x5, waiting for transfers between devices  159 us
    all_gather x1, waiting for transfers between devices, per_device(): lax.all_gather(qry_tan, 'ent', axis=0, tiled=True)  153 us
    all_gather x1, waiting for transfers between devices, per_device(): lax.all_gather(qry_emb, 'ent', axis=0, tiled=True)  146 us
    reduce_scatter x1, waiting for transfers between devices, per_device(): lax.psum_scatter(jnp.concatenate([dot_tn(uhess, queries), dot_tn(ugrad, q...  75 us
    dot_general x3, matrix products, dot_nt(): lax.dot_general(a, b, (((1,), (1,)), ((), ())), preferred_element_type=jn...  21.7 us
  transfers between devices with their start and end apart: 4, of which 4 were waited for; matrix products, arithmetic and copies ran while one was open for 3% of the time, Pallas kernels for 0%

commit v1 on v0

v1 whole, which is shorter than its diff:
```python
import jax
import jax.numpy as jnp
from jax import lax
from jax.experimental import pallas as pl
from jax.experimental.pallas import tpu as pltpu
from jax.sharding import PartitionSpec as P

MESH = pl.DeviceIdType.MESH
F32 = jnp.float32
BF16 = jnp.bfloat16
I32 = jnp.int32
I16 = jnp.int16
D = 512
PLANE = 256
SUB = 512
NEAR_FIRST = (1, 3, 2)
GNVP, GRAD = 0, 1

A_Y, A_X0, A_X1, A_Z0, A_Z1, A_ZZ, A_XX, A_N = 0, 2, 6, 10, 14, 18, 34, 50


def dot_nt(a, b):
    return lax.dot_general(a, b, (((1,), (1,)), ((), ())), preferred_element_type=F32)


def dot_tn(a, b):
    return lax.dot_general(a, b, (((0,), (0,)), ((), ())), preferred_element_type=F32)


def dot_nn(a, b):
    return lax.dot_general(a, b, (((1,), (0,)), ((), ())), preferred_element_type=F32)


def quantize(value, code_ref, scale_ref):
    top = jnp.max(jnp.abs(value), axis=(0, 1), keepdims=True)
    top = jnp.maximum(top, 1e-30)
    code_ref[...] = jnp.round(value * (32767.0 / top)).astype(I32).astype(I16)
    scale_ref[...] = jnp.broadcast_to(top * (1.0 / 32767.0), (8, 128))


def dequantize(code_ref, scale_ref):
    return code_ref[...].astype(I32).astype(F32) * scale_ref[0:1, 0:1]


def kernel(
    ent_hbm,
    ett_hbm,
    q_hbm,
    dq_hbm,
    tails_hbm,
    oeh,
    oeg,
    oqh,
    oqg,
    ent,
    ett,
    qp,
    dqp,
    tails,
    tb,
    w,
    qacc,
    eacc,
    drecv,
    csend,
    crecv,
    cssend,
    csrecv,
    b1s,
    b1r,
    b1ss,
    b1sr,
    b2s,
    b2r,
    b2ss,
    b2sr,
    b3s,
    b3r,
    lsem,
    asend,
    arecv,
    dsend,
    drsem,
    cs_sem,
    cr_sem,
    css_sem,
    csr_sem,
    b1s_sem,
    b1r_sem,
    b1ss_sem,
    b1sr_sem,
    b2s_sem,
    b2r_sem,
    b2ss_sem,
    b2sr_sem,
    b3s_sem,
    b3r_sem,
):
    e_idx = lax.axis_index("ent")
    q_idx = lax.axis_index("qry")
    x, z, yl = e_idx // 8, (e_idx // 2) % 4, e_idx % 2
    yh, c = q_idx // 2, q_idx % 2

    def at(xx, zz, yy):
        return ((xx * 4 + zz) * 2 + yy, q_idx)

    def px(d):
        return at((x + d) % 4, z, yl)

    def pz(d):
        return at(x, (z + d) % 4, yl)

    py = at(x, z, 1 - yl)
    pcore = (e_idx, yh * 2 + 1 - c)
    phi = (e_idx, (1 - yh) * 2 + c)

    started = []

    def send(src, dst, ss, rs, peer):
        cp = pltpu.make_async_remote_copy(
            src_ref=src, dst_ref=dst, send_sem=ss, recv_sem=rs, device_id=peer, device_id_type=MESH
        )
        cp.start()
        started.append(cp)

    def arrived(dst, ss, rs):
        pltpu.make_async_remote_copy(
            src_ref=dst, dst_ref=dst, send_sem=ss, recv_sem=rs, device_id=py, device_id_type=MESH
        ).wait_recv()

    def rows(start, size, step):
        return pl.ds(pl.multiple_of(start, step), size)

    barrier = pltpu.get_barrier_semaphore()
    for peer in [px(d) for d in (1, 2, 3)] + [pz(d) for d in (1, 2, 3)] + [py, pcore, phi]:
        pl.semaphore_signal(barrier, inc=1, device_id=peer, device_id_type=MESH)

    panel = (qp, dqp)
    own = (q_hbm, dq_hbm)
    my16 = [rows(h * 128 + x * 32 + yl * 16, 16, 16) for h in (0, 1)]
    his16 = [rows(h * 128 + x * 32 + (1 - yl) * 16, 16, 16) for h in (0, 1)]

    local = []
    for a in (0, 1):
        for h in (0, 1):
            cp = pltpu.make_async_copy(
                own[a].at[pl.ds(h * 16, 16)], panel[a].at[z, my16[h]], lsem.at[a * 2 + h]
            )
            cp.start()
            local.append(cp)
    for i, (src, dst) in enumerate(((tails_hbm, tails), (ent_hbm, ent), (ett_hbm, ett))):
        cp = pltpu.make_async_copy(src, dst, lsem.at[4 + i])
        cp.start()
        local.append(cp)
    for cp in local[:4]:
        cp.wait()
    pl.semaphore_wait(barrier, 9)

    def slot(a, i):
        return asend.at[a, i], arecv.at[a, i]

    def first_sends(a):
        for h in (0, 1):
            here = panel[a].at[z, my16[h]]
            send(here, here, *slot(a, A_Y + h), py)
        for d in NEAR_FIRST:
            here = panel[a].at[z, my16[0]]
            send(here, here, *slot(a, A_X0 + d), px(d))
            here = panel[a].at[z, my16[1]]
            send(here, here, *slot(a, A_Z0 + d), pz(d))

    def relay_z(a, j):
        here = panel[a].at[z, rows(((x + j) % 4) * 32, 32, 32)]
        for d in NEAR_FIRST:
            send(here, here, *slot(a, A_ZZ + j * 4 + d), pz(d))

    def relay_x(a, j):
        here = panel[a].at[(z + j) % 4, rows(128 + x * 32, 32, 32)]
        for d in NEAR_FIRST:
            send(here, here, *slot(a, A_XX + j * 4 + d), px(d))

    def second_sends(a):
        for h in (0, 1):
            arrived(panel[a].at[z, his16[h]], *slot(a, A_Y + h))
        for d in NEAR_FIRST:
            here = panel[a].at[z, his16[0]]
            send(here, here, *slot(a, A_X1 + d), px(d))
            here = panel[a].at[z, his16[1]]
            send(here, here, *slot(a, A_Z1 + d), pz(d))
        relay_z(a, 0)
        relay_x(a, 0)

    def relays(a):
        for d in NEAR_FIRST:
            for k in (0, 1):
                there = panel[a].at[z, rows(((x - d + 4) % 4) * 32 + k * 16, 16, 16)]
                arrived(there, *slot(a, (A_X0, A_X1)[k] + d))
            relay_z(a, (4 - d) % 4)
            for k in (0, 1):
                there = panel[a].at[(z - d + 4) % 4, rows(128 + x * 32 + k * 16, 16, 16)]
                arrived(there, *slot(a, (A_Z0, A_Z1)[k] + d))
            relay_x(a, (4 - d) % 4)

    def plane_arrived(a, j):
        p = (z + j) % 4
        if j:
            for i in range(4):
                there = panel[a].at[p, rows(((x + i) % 4) * 32, 32, 32)]
                arrived(there, *slot(a, A_ZZ + i * 4 + (4 - j)))
        for d in NEAR_FIRST:
            there = panel[a].at[p, rows(128 + ((x - d + 4) % 4) * 32, 32, 32)]
            arrived(there, *slot(a, A_XX + j * 4 + d))

    first_sends(0)
    first_sends(1)

    def clear(i, _):
        eacc[0, rows(i * 128, 128, 128)] = jnp.zeros((128, D), F32)
        eacc[1, rows(i * 128, 128, 128)] = jnp.zeros((128, D), F32)
        return 0

    lax.fori_loop(0, 16, clear, 0)
    second_sends(0)

    local[4].wait()

    def spread(i, _):
        xx, zz, yy = i // 8, (i // 2) % 4, i % 2
        for h in (0, 1):
            t = tails[rows(i * 32 + h * 16, 16, 16)] - e_idx * (4 * SUB)
            for k in range(4):
                tb[k, zz, rows(h * 128 + xx * 32 + yy * 16, 16, 16)] = jnp.broadcast_to(
                    t[:, k : k + 1], (16, 128)
                )
        return 0

    lax.fori_loop(0, 32, spread, 0)

    def clear_q(i, _):
        qacc[0, i] = jnp.zeros((PLANE, D), F32)
        qacc[1, i] = jnp.zeros((PLANE, D), F32)
        return 0

    lax.fori_loop(0, 4, clear_q, 0)
    relays(0)
    second_sends(1)
    local[5].wait()

    def grad_tile(p, s):
        es = rows(s * SUB, SUB, SUB)
        q = qp[p]
        e = ent[es]
        score = dot_nt(q, e)
        lane = lax.broadcasted_iota(I32, (PLANE, 128), 1)
        label = []
        for b in range(SUB // 128):
            ids = lane + (s * SUB + b * 128)
            hit = tb[0, p] == ids
            for k in range(1, 4):
                hit = hit | (tb[k, p] == ids)
            label.append(jnp.where(hit, 1.0, 0.0).astype(F32))
        label = jnp.concatenate(label, axis=1)
        prob = 1.0 / (1.0 + jnp.exp(-score))
        w[p, s] = prob * (1.0 - prob)
        ugrad = (prob - label).astype(BF16)
        qacc[GRAD, p] += dot_nn(ugrad, e)
        eacc[GRAD, es] += dot_tn(ugrad, q)

    def gnvp_tile(p, s):
        es = rows(s * SUB, SUB, SUB)
        q = qp[p]
        e = ent[es]
        dscore = dot_nt(dqp[p], e) + dot_nt(q, ett[es])
        uhess = (w[p, s] * dscore).astype(BF16)
        qacc[GNVP, p] += dot_nn(uhess, e)
        eacc[GNVP, es] += dot_tn(uhess, q)

    far_other = (1 - yh) * 2 + 1 - c
    far_same = (1 - yh) * 2 + c
    near_other = yh * 2 + 1 - c
    near_same = yh * 2 + c

    def both(tile, j, far):
        p = (z + j) % 4
        base = (1 - yh if far else yh) * 2

        def step(i, _):
            tile(p, base + (1 - c + i) % 2)
            return 0

        lax.fori_loop(0, 2, step, 0)

    def to_core(k, i, s):
        for b in (0, 1):
            send(
                eacc.at[k, rows(s * SUB + b * 256, 256, 256)],
                drecv.at[k, i, pl.ds(b * 256, 256)],
                dsend.at[k, i, b],
                drsem.at[k, i, b],
                pcore,
            )

    def to_far(k):
        for b in (0, 1):
            here = drecv.at[k, 0, pl.ds(b * 256, 256)]
            arrived(here, dsend.at[k, 0, b], drsem.at[k, 0, b])
            value = eacc[k, rows(far_same * SUB + b * 256, 256, 256)] + here[...]
            quantize(value, csend.at[k, b], cssend.at[k, b])
            send(csend.at[k, b], crecv.at[k, b], cs_sem.at[k, b], cr_sem.at[k, b], phi)
            send(cssend.at[k, b], csrecv.at[k, b], css_sem.at[k, b], csr_sem.at[k, b], phi)

    def finish_entities(k, out):
        for b in (0, 1):
            here = drecv.at[k, 1, pl.ds(b * 256, 256)]
            arrived(here, dsend.at[k, 1, b], drsem.at[k, 1, b])
            arrived(csrecv.at[k, b], css_sem.at[k, b], csr_sem.at[k, b])
            arrived(crecv.at[k, b], cs_sem.at[k, b], cr_sem.at[k, b])
            out[pl.ds(b * 256, 256)] = (
                eacc[k, rows(near_same * SUB + b * 256, 256, 256)]
                + here[...]
                + dequantize(crecv.at[k, b], csrecv.at[k, b])
            )

    def to_1(k, d, value, peer):
        i = d - 1
        quantize(value, b1s.at[k, i], b1ss.at[k, i])
        send(b1ss.at[k, i], b1sr.at[k, i], b1ss_sem.at[k, i], b1sr_sem.at[k, i], peer)
        send(b1s.at[k, i], b1r.at[k, i], b1s_sem.at[k, i], b1r_sem.at[k, i], peer)

    def of_1(k, i):
        arrived(b1sr.at[k, i], b1ss_sem.at[k, i], b1sr_sem.at[k, i])
        arrived(b1r.at[k, i], b1s_sem.at[k, i], b1r_sem.at[k, i])
        return dequantize(b1r.at[k, i], b1sr.at[k, i])

    def to_2(k, d, value, peer):
        i = d - 1
        quantize(value, b2s.at[k, i], b2ss.at[k, i])
        send(b2ss.at[k, i], b2sr.at[k, i], b2ss_sem.at[k, i], b2sr_sem.at[k, i], peer)
        send(b2s.at[k, i], b2r.at[k, i], b2s_sem.at[k, i], b2r_sem.at[k, i], peer)

    def of_2(k, i):
        arrived(b2sr.at[k, i], b2ss_sem.at[k, i], b2sr_sem.at[k, i])
        arrived(b2r.at[k, i], b2s_sem.at[k, i], b2r_sem.at[k, i])
        return dequantize(b2r.at[k, i], b2sr.at[k, i])

    def column(k, p, xx):
        return jnp.concatenate([qacc[k, p, rows(h * 128 + xx * 32, 32, 32)] for h in (0, 1)], axis=0)

    def to_3(k, total):
        b3s[k] = total
        for h in (0, 1):
            send(
                b3s.at[k, rows(h * 32 + (1 - yl) * 16, 16, 16)],
                b3r.at[k, pl.ds(h * 16, 16)],
                b3s_sem.at[k, h],
                b3r_sem.at[k, h],
                py,
            )

    def finish_queries(k, out):
        for h in (0, 1):
            arrived(b3r.at[k, pl.ds(h * 16, 16)], b3s_sem.at[k, h], b3r_sem.at[k, h])
            out[pl.ds(h * 16, 16)] = b3s[k, rows(h * 32 + yl * 16, 16, 16)] + b3r[k, pl.ds(h * 16, 16)]

    for j in (0, 1, 3):
        plane_arrived(0, j)
        both(grad_tile, j, True)
    plane_arrived(0, 2)
    grad_tile((z + 2) % 4, far_other)
    to_core(GRAD, 0, far_other)
    grad_tile((z + 2) % 4, far_same)
    relays(1)
    both(grad_tile, 0, False)
    to_far(GRAD)

    def near_grad(i, _):
        p = (z + i) % 4
        grad_tile(p, near_other)
        grad_tile(p, near_same)
        return 0

    lax.fori_loop(1, 4, near_grad, 0)
    to_core(GRAD, 1, near_other)
    for d in NEAR_FIRST:
        value = jnp.concatenate([column(GRAD, p, (x + d) % 4) for p in range(4)], axis=0)
        to_1(GRAD, d, value, px(d))
    local[6].wait()
    for j in (0, 1, 3):
        plane_arrived(1, j)
        both(gnvp_tile, j, True)
    plane_arrived(1, 2)
    gnvp_tile((z + 2) % 4, far_other)
    to_core(GNVP, 0, far_other)
    gnvp_tile((z + 2) % 4, far_same)
    both(gnvp_tile, 1, False)
    to_far(GNVP)
    to_1(GNVP, 1, qacc[GNVP, (z + 1) % 4], pz(1))
    both(gnvp_tile, 3, False)
    to_1(GNVP, 3, qacc[GNVP, (z + 3) % 4], pz(3))
    both(gnvp_tile, 2, False)
    to_1(GNVP, 2, qacc[GNVP, (z + 2) % 4], pz(2))
    total = jnp.concatenate([column(GRAD, p, x) for p in range(4)], axis=0)
    for i in range(3):
        total = total + of_1(GRAD, i)
    for p in range(4):
        w[0, far_same, pl.ds(p * 64, 64)] = total[p * 64 : (p + 1) * 64]
    for d in NEAR_FIRST:
        to_2(GRAD, d, w[0, far_same, rows(((z + d) % 4) * 64, 64, 64)], pz(d))
    both(gnvp_tile, 0, False)
    to_core(GNVP, 1, near_other)
    total = qacc[GNVP, z]
    for i in range(3):
        total = total + of_1(GNVP, i)
    qacc[GNVP, z] = total
    for d in NEAR_FIRST:
        to_2(GNVP, d, column(GNVP, z, (x + d) % 4), px(d))
    total = w[0, far_same, rows(z * 64, 64, 64)]
    for i in range(3):
        total = total + of_2(GRAD, i)
    to_3(GRAD, total)
    total = column(GNVP, z, x)
    for i in range(3):
        total = total + of_2(GNVP, i)
    to_3(GNVP, total)
    finish_queries(GRAD, oqg)
    finish_queries(GNVP, oqh)
    finish_entities(GRAD, oeg)
    finish_entities(GNVP, oeh)
    for cp in started:
        cp.wait_send()


def per_device(ent_emb, ent_tan, qry_emb, qry_tan, tails):
    any_space = pl.BlockSpec(memory_space=pl.ANY)
    vmem = pl.BlockSpec(memory_space=pltpu.VMEM)
    dma = pltpu.SemaphoreType.DMA
    outs = (
        jax.ShapeDtypeStruct((SUB, D), F32),
        jax.ShapeDtypeStruct((SUB, D), F32),
        jax.ShapeDtypeStruct((32, D), F32),
        jax.ShapeDtypeStruct((32, D), F32),
    )
    return pl.pallas_call(
        kernel,
        out_shape=outs,
        in_specs=[any_space] * 5,
        out_specs=[vmem] * 4,
        scratch_shapes=[
            pltpu.VMEM((4 * SUB, D), BF16),
            pltpu.VMEM((4 * SUB, D), BF16),
            pltpu.VMEM((4, PLANE, D), BF16),
            pltpu.VMEM((4, PLANE, D), BF16),
            pltpu.VMEM((4 * PLANE, 4), I32),
            pltpu.VMEM((4, 4, PLANE, 128), I32),
            pltpu.VMEM((4, 4, PLANE, SUB), F32),
            pltpu.VMEM((2, 4, PLANE, D), F32),
            pltpu.VMEM((2, 4 * SUB, D), F32),
            pltpu.VMEM((2, 2, SUB, D), F32),
            pltpu.VMEM((2, 2, 256, D), I16),
            pltpu.VMEM((2, 2, 256, D), I16),
            pltpu.VMEM((2, 2, 8, 128), F32),
            pltpu.VMEM((2, 2, 8, 128), F32),
            pltpu.VMEM((2, 3, PLANE, D), I16),
            pltpu.VMEM((2, 3, PLANE, D), I16),
            pltpu.VMEM((2, 3, 8, 128), F32),
            pltpu.VMEM((2, 3, 8, 128), F32),
            pltpu.VMEM((2, 3, 64, D), I16),
            pltpu.VMEM((2, 3, 64, D), I16),
            pltpu.VMEM((2, 3, 8, 128), F32),
            pltpu.VMEM((2, 3, 8, 128), F32),
            pltpu.VMEM((2, 64, D), F32),
            pltpu.VMEM((2, 32, D), F32),
            dma((7,)),
            dma((2, A_N)),
            dma((2, A_N)),
            dma((2, 2, 2)),
            dma((2, 2, 2)),
            dma((2, 2)),
            dma((2, 2)),
            dma((2, 2)),
            dma((2, 2)),
            dma((2, 3)),
            dma((2, 3)),
            dma((2, 3)),
            dma((2, 3)),
            dma((2, 3)),
            dma((2, 3)),
            dma((2, 3)),
            dma((2, 3)),
            dma((2, 2)),
            dma((2, 2)),
        ],
        compiler_params=pltpu.CompilerParams(
            collective_id=0, has_side_effects=True, vmem_limit_bytes=60 * 2**20
        ),
    )(ent_emb, ent_tan, qry_emb, qry_tan, tails)


def solution(mesh):
    return jax.shard_map(
        per_device,
        mesh=mesh,
        in_specs=(
            P("ent", None),
            P("ent", None),
            P(("qry", "ent"), None),
            P(("qry", "ent"), None),
            P("qry", None),
        ),
        out_specs=(
            P(("ent", "qry"), None),
            P(("ent", "qry"), None),
            P(("qry", "ent"), None),
            P(("qry", "ent"), None),
        ),
        check_vma=False,
    )
```

time: 607 us -> 76.7 us (0.13)
  waiting for transfers between devices: 534 us -> 0 us
  Pallas kernels: 0 us -> 69.2 us
  matrix products: 36.1 us -> 0 us
  between operations: 13.8 us -> 0.67 us
  local copies, waits for them, and re-layouts: 15.4 us -> 6.33 us
  other arithmetic: 6.33 us -> 0 us
    all_gather x2 -> x0, waiting for transfers between devices: 299 us -> none  [the longest x1 153 us: per_device(): lax.all_gather(qry_tan, 'ent', axis=0, tiled=True)]
    unnamed x5 -> x0, waiting for transfers between devices: 159 us -> none
    reduce_scatter x1 -> x0, waiting for transfers between devices: 75 us -> none  [per_device(): lax.psum_scatter(jnp.concatenate([dot_tn(uhess, queries), dot_tn(ugrad, q...]
    pallas_call x0 -> x1, Pallas kernels: none -> 69.2 us  [per_device(): pl.pallas_call(kernel, out_shape=outs, in_specs=[any_space] * 5, out_spec...]
    dot_general x7 -> x0, matrix products: 36.1 us -> none  [the longest x3 21.7 us: dot_nt(): lax.dot_general(a, b, (((1,), (1,)), ((), ())), preferred_element_type=jn...]
    concatenate x2 -> x0, other arithmetic: 6.32 us -> none  [the longest x1 3.81 us: per_device(): jnp.concatenate([dot_tn(uhess, queries), dot_tn(ugrad, queries)], axis=1)]
  transfers between devices with their start and end apart: 4 -> 0, of which waited for: 4 -> 0; matrix products, arithmetic and copies ran while one was open for 3% -> 0% of each run, Pallas kernels for 0% -> 0%
where the time goes in v1:
time: 76.7 us; the launch traced here: 76.2 us
  Pallas kernels  69.2 us (90%)
  local copies, waits for them, and re-layouts  6.33 us (8%)
    pallas_call x1, Pallas kernels, per_device(): pl.pallas_call(kernel, out_shape=outs, in_specs=[any_space] * 5, out_spec...  69.2 us
    unnamed x11, local copies, waits for them, and re-layouts  6.33 us

profile of v1, /device:TPU:0, one launch (start us, length us, event | category | flops | bytes accessed | tf_op | source)
XLA Modules:
  0.0 76.2 jit_solution(12753013989797598717)
XLA Ops:
  0.6 1.7 %copy.9.tails_hbm = s32[1024,4]{1,0:T(8,128)} copy(s32[1024,4]{0,1:T(4,128)} %param.9) | data formatting | bytes 32768 | tf_op args[4]
  2.4 69.2 %shard_map.84 = (f32[512,512]{1,0:T(8,128)}, f32[512,512]{1,0:T(8,128)}, f32[32,512]{1,0:T(8,128)}, f32[32,512]{1,0:T(8,128)}) custom-call(bf16[2048,512]{1,0:T(8,128)(2,1)} %ent_hbm.1, bf16[2048,512]{1,0:T(8,128)(2,1)} %ett_hbm.1, bf16[32,512]{1,0:T(8,128)(2,1)} %q_hbm.1, bf16[32,512]{1,0:T(8,128)(2,1)} %dq_hbm.1, s32[1024,4]{1,0:T(8,128)} %copy.9.tails_hbm), custom_call_target="tpu_custom_call" | custom-call | tf_op jit(solution)/shard_map/pallas_call | solution.py:443
  71.6 0.0 copy-start
  71.6 0.0 copy-start.2
  71.6 0.0 copy-start.1
  71.7 2.4 %copy.14 = f32[512,512]{1,0:T(8,128)} copy(f32[512,512]{1,0:T(8,128)} %get-tuple-element.8) | data formatting | bytes 2097152
  74.0 0.0 copy-done
  74.0 1.0 %copy.15 = f32[512,512]{1,0:T(8,128)} copy(f32[512,512]{1,0:T(8,128)S(1)} %copy-done) | data formatting | bytes 2097152
  75.0 0.0 copy-done.2
  75.0 0.6 copy.16
  75.6 0.0 copy-done.1
  75.6 0.6 copy.17
Async XLA Ops:
  71.6 2.4 %copy-start = (f32[512,512]{1,0:T(8,128)S(1)}, f32[512,512]{1,0:T(8,128)}, u32[]{:S(2)}) copy-start(f32[512,512]{1,0:T(8,128)} %get-tuple-element.9) | copy-start | bytes 3145732
  71.6 3.4 %copy-start.2 = (f32[32,512]{1,0:T(8,128)S(1)}, f32[32,512]{1,0:T(8,128)}, u32[]{:S(2)}) copy-start(f32[32,512]{1,0:T(8,128)} %get-tuple-element.10) | copy-start | bytes 196612
  71.6 4.0 %copy-start.1 = (f32[32,512]{1,0:T(8,128)S(1)}, f32[32,512]{1,0:T(8,128)}, u32[]{:S(2)}) copy-start(f32[32,512]{1,0:T(8,128)} %get-tuple-element.11) | copy-start | bytes 196612

commit v2 on v1

v2 whole, which is shorter than its diff:
```python
import jax
import jax.numpy as jnp
from jax import lax
from jax.experimental import pallas as pl
from jax.experimental.pallas import tpu as pltpu
from jax.sharding import PartitionSpec as P

MESH = pl.DeviceIdType.MESH
F32 = jnp.float32
BF16 = jnp.bfloat16
I32 = jnp.int32
I16 = jnp.int16
D = 512
PLANE = 256
SUB = 512
NEAR_FIRST = (1, 3, 2)
VMEM_LIMIT = 50 * 2**20
GNVP, GRAD = 0, 1

A_X, A_Z, A_ZZ, A_XX, A_N = 0, 8, 16, 32, 48


def dot_nt(a, b):
    return lax.dot_general(a, b, (((1,), (1,)), ((), ())), preferred_element_type=F32)


def dot_tn(a, b):
    return lax.dot_general(a, b, (((0,), (0,)), ((), ())), preferred_element_type=F32)


def dot_nn(a, b):
    return lax.dot_general(a, b, (((1,), (0,)), ((), ())), preferred_element_type=F32)


def quantize(value, code_ref, scale_ref):
    top = jnp.max(jnp.abs(value), axis=(0, 1), keepdims=True)
    top = jnp.maximum(top, 1e-30)
    code_ref[...] = jnp.round(value * (32767.0 / top)).astype(I32).astype(I16)
    scale_ref[...] = jnp.broadcast_to(top * (1.0 / 32767.0), (8, 128))


def dequantize(code_ref, scale_ref):
    return code_ref[...].astype(I32).astype(F32) * scale_ref[0:1, 0:1]


def kernel(
    ent_hbm,
    ett_hbm,
    q_hbm,
    dq_hbm,
    tails_hbm,
    oeh,
    oeg,
    oqh,
    oqg,
    ent,
    ett,
    qp,
    dqp,
    tails,
    tb,
    w,
    qacc,
    eacc,
    drecv,
    csend,
    crecv,
    cssend,
    csrecv,
    bq,
    bqs,
    br0,
    br0s,
    br1,
    br1s,
    b2s,
    b2r,
    b3s,
    b3r,
    lsem,
    asend,
    arecv,
    dsend,
    drsem,
    cs_sem,
    cr_sem,
    css_sem,
    csr_sem,
    b0_ss,
    b0_rs,
    b0s_ss,
    b0s_rs,
    b1_ss,
    b1_rs,
    b1s_ss,
    b1s_rs,
    b2_ss,
    b2_rs,
    b3_ss,
    b3_rs,
):
    e_idx = lax.axis_index("ent")
    q_idx = lax.axis_index("qry")
    x, z, yl = e_idx // 8, (e_idx // 2) % 4, e_idx % 2
    yh, c = q_idx // 2, q_idx % 2

    def at(xx, zz, yy):
        return ((xx * 4 + zz) * 2 + yy, q_idx)

    def px(d, dy=0):
        return at((x + d) % 4, z, (yl + dy) % 2)

    def pz(d, dy=0):
        return at(x, (z + d) % 4, (yl + dy) % 2)

    py = at(x, z, 1 - yl)
    pcore = (e_idx, yh * 2 + 1 - c)
    phi = (e_idx, (1 - yh) * 2 + c)

    started = []

    def send(src, dst, ss, rs, peer):
        cp = pltpu.make_async_remote_copy(
            src_ref=src, dst_ref=dst, send_sem=ss, recv_sem=rs, device_id=peer, device_id_type=MESH
        )
        cp.start()
        started.append(cp)

    def arrived(dst, ss, rs):
        pltpu.make_async_remote_copy(
            src_ref=dst, dst_ref=dst, send_sem=ss, recv_sem=rs, device_id=py, device_id_type=MESH
        ).wait_recv()

    def rows(start, size, step):
        return pl.ds(pl.multiple_of(start, step), size)

    barrier = pltpu.get_barrier_semaphore()
    sides = [(d, dy) for d in (1, 2, 3) for dy in (0, 1)]
    for peer in [px(*s) for s in sides] + [pz(*s) for s in sides] + [py, pcore, phi]:
        pl.semaphore_signal(barrier, inc=1, device_id=peer, device_id_type=MESH)

    panel = (qp, dqp)
    own = (q_hbm, dq_hbm)
    my16 = [rows(h * 128 + x * 32 + yl * 16, 16, 16) for h in (0, 1)]

    local = []
    for a in (0, 1):
        for h in (0, 1):
            cp = pltpu.make_async_copy(
                own[a].at[pl.ds(h * 16, 16)], panel[a].at[z, my16[h]], lsem.at[a * 2 + h]
            )
            cp.start()
            local.append(cp)
    for i, (src, dst) in enumerate(((tails_hbm, tails), (ent_hbm, ent), (ett_hbm, ett))):
        cp = pltpu.make_async_copy(src, dst, lsem.at[4 + i])
        cp.start()
        local.append(cp)
    for cp in local[:4]:
        cp.wait()
    pl.semaphore_wait(barrier, 15)

    def slot(a, i):
        return asend.at[a, i], arecv.at[a, i]

    def first_sends(a):
        here = [panel[a].at[z, my16[h]] for h in (0, 1)]
        send(here[0], here[0], *slot(a, A_X + 1), py)
        send(here[1], here[1], *slot(a, A_Z + 1), py)
        for d in NEAR_FIRST:
            for dy in (0, 1):
                send(here[0], here[0], *slot(a, A_X + d * 2 + dy), px(d, dy))
                send(here[1], here[1], *slot(a, A_Z + d * 2 + dy), pz(d, dy))

    def first_arrived(a, d):
        for dy in (0, 1) if d else (1,):
            k = (yl + dy) % 2 * 16
            there = panel[a].at[z, rows(((x - d + 4) % 4) * 32 + k, 16, 16)]
            arrived(there, *slot(a, A_X + d * 2 + dy))
            there = panel[a].at[(z - d + 4) % 4, rows(128 + x * 32 + k, 16, 16)]
            arrived(there, *slot(a, A_Z + d * 2 + dy))

    def relays(a):
        for d in (0,) + NEAR_FIRST:
            first_arrived(a, d)
            j = (4 - d) % 4
            here = panel[a].at[z, rows(((x + j) % 4) * 32, 32, 32)]
            for e in NEAR_FIRST:
                send(here, here, *slot(a, A_ZZ + j * 4 + e), pz(e))
            here = panel[a].at[(z + j) % 4, rows(128 + x * 32, 32, 32)]
            for e in NEAR_FIRST:
                send(here, here, *slot(a, A_XX + j * 4 + e), px(e))

    def plane_arrived(a, j):
        p = (z + j) % 4
        if j:
            for i in range(4):
                there = panel[a].at[p, rows(((x + i) % 4) * 32, 32, 32)]
                arrived(there, *slot(a, A_ZZ + i * 4 + (4 - j)))
        for d in NEAR_FIRST:
            there = panel[a].at[p, rows(128 + ((x - d + 4) % 4) * 32, 32, 32)]
            arrived(there, *slot(a, A_XX + j * 4 + d))

    first_sends(0)
    first_sends(1)

    local[4].wait()

    def spread(m, _):
        for k in range(4):
            t = tails[pl.ds(k, 1), pl.ds(pl.multiple_of(m * 128, 128), 128)] - e_idx * (4 * SUB)
            t = jnp.broadcast_to(t, (128, 128)).T
            for i in range(8):
                to = rows(i % 2 * 128 + m // 2 * 32 + i // 2 % 2 * 16, 16, 16)
                tb[k, m % 2 * 2 + i // 4, to] = t[i * 16 : (i + 1) * 16]
        return 0

    lax.fori_loop(0, 8, spread, 0)
    relays(0)
    relays(1)
    local[5].wait()

    def add(ref, value, first):
        ref[...] = value if first else ref[...] + value

    def grad_tile(j, far, first):
        p = (z + j) % 4
        half = 1 - yh if far else yh
        es = rows(half * 2 * SUB, 2 * SUB, 2 * SUB)
        q = qp[p]
        e = ent[es]
        score = dot_nt(q, e)
        lane = lax.broadcasted_iota(I32, (PLANE, 128), 1)
        label = []
        for b in range(2 * SUB // 128):
            ids = lane + (half * 2 * SUB + b * 128)
            hit = tb[0, p] == ids
            for k in range(1, 4):
                hit = hit | (tb[k, p] == ids)
            label.append(jnp.where(hit, 1.0, 0.0).astype(F32))
        label = jnp.concatenate(label, axis=1)
        prob = 1.0 / (1.0 + jnp.exp(-score))
        w[half, p] = prob * (1.0 - prob)
        ugrad = (prob - label).astype(BF16)
        add(qacc.at[GRAD, p], dot_nn(ugrad, e), far)
        add(eacc.at[GRAD, es], dot_tn(ugrad, q), first)

    def gnvp_tile(j, far, first):
        p = (z + j) % 4
        half = 1 - yh if far else yh
        es = rows(half * 2 * SUB, 2 * SUB, 2 * SUB)
        q = qp[p]
        e = ent[es]
        dscore = dot_nt(
            jnp.concatenate([dqp[p], q], axis=1), jnp.concatenate([e, ett[es]], axis=1)
        )
        uhess = (w[half, p] * dscore).astype(BF16)
        add(qacc.at[GNVP, p], dot_nn(uhess, e), far)
        add(eacc.at[GNVP, es], dot_tn(uhess, q), first)

    far_other = (1 - yh) * 2 + 1 - c
    far_same = (1 - yh) * 2 + c
    near_other = yh * 2 + 1 - c
    near_same = yh * 2 + c

    def to_core(k, i, s):
        for b in (0, 1):
            send(
                eacc.at[k, rows(s * SUB + b * 256, 256, 256)],
                drecv.at[k, i, pl.ds(b * 256, 256)],
                dsend.at[k, i, b],
                drsem.at[k, i, b],
                pcore,
            )

    def to_far(k):
        for b in (0, 1):
            here = drecv.at[k, 0, pl.ds(b * 256, 256)]
            arrived(here, dsend.at[k, 0, b], drsem.at[k, 0, b])
            value = eacc[k, rows(far_same * SUB + b * 256, 256, 256)] + here[...]
            quantize(value, csend.at[k, b], cssend.at[k, b])
            send(csend.at[k, b], crecv.at[k, b], cs_sem.at[k, b], cr_sem.at[k, b], phi)
            send(cssend.at[k, b], csrecv.at[k, b], css_sem.at[k, b], csr_sem.at[k, b], phi)

    def finish_entities(k, out):
        for b in (0, 1):
            here = drecv.at[k, 1, pl.ds(b * 256, 256)]
            arrived(here, dsend.at[k, 1, b], drsem.at[k, 1, b])
            arrived(csrecv.at[k, b], css_sem.at[k, b], csr_sem.at[k, b])
            arrived(crecv.at[k, b], cs_sem.at[k, b], cr_sem.at[k, b])
            out[pl.ds(b * 256, 256)] = (
                eacc[k, rows(near_same * SUB + b * 256, 256, 256)]
                + here[...]
                + dequantize(crecv.at[k, b], csrecv.at[k, b])
            )

    def to_1(k, j):
        p = (z + j) % 4
        quantize(qacc[k, p], bq.at[k, j], bqs.at[k, j])
        if j:
            send(bqs.at[k, j], br0s.at[k, j], b0s_ss.at[k, j], b0s_rs.at[k, j], pz(j))
            here = bq.at[k, j, pl.ds(0, 128)]
            send(here, br0.at[k, j], b0_ss.at[k, j], b0_rs.at[k, j], pz(j))
        for d in NEAR_FIRST:
            send(bqs.at[k, j], br1s.at[k, j, d], b1s_ss.at[k, j, d], b1s_rs.at[k, j, d], px(d))
            here = bq.at[k, j, rows(128 + ((x + d) % 4) * 32, 32, 32)]
            send(here, br1.at[k, j, d], b1_ss.at[k, j, d], b1_rs.at[k, j, d], px(d))

    def to_2(k):
        total = qacc[k, z, pl.ds(0, 128)]
        for j in NEAR_FIRST:
            arrived(br0s.at[k, j], b0s_ss.at[k, j], b0s_rs.at[k, j])
            arrived(br0.at[k, j], b0_ss.at[k, j], b0_rs.at[k, j])
            total = total + dequantize(br0.at[k, j], br0s.at[k, j])
        b2s[k, 0] = total
        for d in NEAR_FIRST:
            here = b2s.at[k, 0, rows(((x + d) % 4) * 32, 32, 32)]
            send(here, b2r.at[k, d], b2_ss.at[k, d], b2_rs.at[k, d], px(d))
        for j in (2, 1, 3, 0):
            total = qacc[k, (z + j) % 4, rows(128 + x * 32, 32, 32)]
            for d in NEAR_FIRST:
                arrived(br1s.at[k, j, d], b1s_ss.at[k, j, d], b1s_rs.at[k, j, d])
                arrived(br1.at[k, j, d], b1_ss.at[k, j, d], b1_rs.at[k, j, d])
                total = total + dequantize(br1.at[k, j, d], br1s.at[k, j, d])
            b2s[k, 1, pl.ds(j * 32, 32)] = total
            if j:
                here = b2s.at[k, 1, pl.ds(j * 32, 32)]
                send(here, b2r.at[k, 4 + j], b2_ss.at[k, 4 + j], b2_rs.at[k, 4 + j], pz(j))

    def to_3(k):
        for h in (0, 1):
            total = b2s[k, 0, rows(x * 32, 32, 32)] if h == 0 else b2s[k, 1, pl.ds(0, 32)]
            for d in NEAR_FIRST:
                i = h * 4 + d
                arrived(b2r.at[k, i], b2_ss.at[k, i], b2_rs.at[k, i])
                total = total + b2r[k, i]
            b3s[k, h] = total
            here = b3s.at[k, h, rows((1 - yl) * 16, 16, 16)]
            send(here, b3r.at[k, h], b3_ss.at[k, h], b3_rs.at[k, h], py)

    def finish_queries(k, out):
        for h in (0, 1):
            arrived(b3r.at[k, h], b3_ss.at[k, h], b3_rs.at[k, h])
            out[pl.ds(h * 16, 16)] = b3s[k, h, rows(yl * 16, 16, 16)] + b3r[k, h]

    for j in (0,) + NEAR_FIRST:
        plane_arrived(0, j)
        grad_tile(j, True, j == 0)
    to_core(GRAD, 0, far_other)
    grad_tile(2, False, True)
    to_1(GRAD, 2)
    grad_tile(1, False, False)
    to_far(GRAD)
    to_1(GRAD, 1)
    grad_tile(3, False, False)
    to_1(GRAD, 3)
    grad_tile(0, False, False)
    to_1(GRAD, 0)
    to_core(GRAD, 1, near_other)
    local[6].wait()
    for j in (0,) + NEAR_FIRST:
        plane_arrived(1, j)
        gnvp_tile(j, True, j == 0)
    to_core(GNVP, 0, far_other)
    gnvp_tile(2, False, True)
    to_1(GNVP, 2)
    gnvp_tile(1, False, False)
    to_far(GNVP)
    to_1(GNVP, 1)
    to_2(GRAD)
    gnvp_tile(3, False, False)
    to_1(GNVP, 3)
    gnvp_tile(0, False, False)
    to_1(GNVP, 0)
    to_core(GNVP, 1, near_other)
    to_3(GRAD)
    to_2(GNVP)
    finish_queries(GRAD, oqg)
    to_3(GNVP)
    finish_entities(GRAD, oeg)
    finish_queries(GNVP, oqh)
    finish_entities(GNVP, oeh)
    for cp in started:
        cp.wait_send()


def store(a, b, c, d, to_a, to_b, to_c, to_d, sem):
    copies = [
        pltpu.make_async_copy(src, dst, sem.at[i])
        for i, (src, dst) in enumerate(((a, to_a), (b, to_b), (c, to_c), (d, to_d)))
    ]
    for cp in copies:
        cp.start()
    for cp in copies:
        cp.wait()


def per_device(ent_emb, ent_tan, qry_emb, qry_tan, tails):
    any_space = pl.BlockSpec(memory_space=pl.ANY)
    vmem = pl.BlockSpec(memory_space=pltpu.VMEM)
    dma = pltpu.SemaphoreType.DMA
    outs = (
        jax.ShapeDtypeStruct((SUB, D), F32),
        jax.ShapeDtypeStruct((SUB, D), F32),
        jax.ShapeDtypeStruct((32, D), F32),
        jax.ShapeDtypeStruct((32, D), F32),
    )
    results = pl.pallas_call(
        kernel,
        out_shape=outs,
        in_specs=[any_space] * 5,
        out_specs=[vmem] * 4,
        scratch_shapes=[
            pltpu.VMEM((4 * SUB, D), BF16),
            pltpu.VMEM((4 * SUB, D), BF16),
            pltpu.VMEM((4, PLANE, D), BF16),
            pltpu.VMEM((4, PLANE, D), BF16),
            pltpu.VMEM((4, 4 * PLANE), I32),
            pltpu.VMEM((4, 4, PLANE, 128), I32),
            pltpu.VMEM((2, 4, PLANE, 2 * SUB), F32),
            pltpu.VMEM((2, 4, PLANE, D), F32),
            pltpu.VMEM((2, 4 * SUB, D), F32),
            pltpu.VMEM((2, 2, SUB, D), F32),
            pltpu.VMEM((2, 2, 256, D), I16),
            pltpu.VMEM((2, 2, 256, D), I16),
            pltpu.VMEM((2, 2, 8, 128), F32),
            pltpu.VMEM((2, 2, 8, 128), F32),
            pltpu.VMEM((2, 4, PLANE, D), I16),
            pltpu.VMEM((2, 4, 8, 128), F32),
            pltpu.VMEM((2, 4, 128, D), I16),
            pltpu.VMEM((2, 4, 8, 128), F32),
            pltpu.VMEM((2, 4, 4, 32, D), I16),
            pltpu.VMEM((2, 4, 4, 8, 128), F32),
            pltpu.VMEM((2, 2, 128, D), F32),
            pltpu.VMEM((2, 8, 32, D), F32),
            pltpu.VMEM((2, 2, 32, D), F32),
            pltpu.VMEM((2, 2, 16, D), F32),
            dma((7,)),
            dma((2, A_N)),
            dma((2, A_N)),
            dma((2, 2, 2)),
            dma((2, 2, 2)),
            dma((2, 2)),
            dma((2, 2)),
            dma((2, 2)),
            dma((2, 2)),
            dma((2, 4)),
            dma((2, 4)),
            dma((2, 4)),
            dma((2, 4)),
            dma((2, 4, 4)),
            dma((2, 4, 4)),
            dma((2, 4, 4)),
            dma((2, 4, 4)),
            dma((2, 8)),
            dma((2, 8)),
            dma((2, 2)),
            dma((2, 2)),
        ],
        compiler_params=pltpu.CompilerParams(
            collective_id=0, has_side_effects=True, vmem_limit_bytes=VMEM_LIMIT
        ),
    )(ent_emb, ent_tan, qry_emb, qry_tan, tails.T)
    return pl.pallas_call(
        store,
        out_shape=outs,
        in_specs=[vmem] * 4,
        out_specs=[any_space] * 4,
        scratch_shapes=[dma((4,))],
        compiler_params=pltpu.CompilerParams(vmem_limit_bytes=8 * 2**20),
    )(*results)


def solution(mesh):
    return jax.shard_map(
        per_device,
        mesh=mesh,
        in_specs=(
            P("ent", None),
            P("ent", None),
            P(("qry", "ent"), None),
            P(("qry", "ent"), None),
            P("qry", None),
        ),
        out_specs=(
            P(("ent", "qry"), None),
            P(("ent", "qry"), None),
            P(("qry", "ent"), None),
            P(("qry", "ent"), None),
        ),
        check_vma=False,
    )
```

time: 76.7 us -> 65.4 us (0.85)
  Pallas kernels: 69.2 us -> 62 us
  local copies, waits for them, and re-layouts: 6.33 us -> 2.23 us
    pallas_call x1, Pallas kernels: 69.2 us -> 60.6 us  [per_device(): pl.pallas_call(kernel, out_shape=outs, in_specs=[any_space] * 5, out_spec...]
    unnamed x11 -> x6, local copies, waits for them, and re-layouts: 6.33 us -> 2.23 us
    pallas_call x0 -> x1, Pallas kernels: none -> 1.38 us  [per_device(): pl.pallas_call(store, out_shape=outs, in_specs=[vmem] * 4, out_specs=[any...]
where the time goes in v2:
time: 65.4 us; the launch traced here: 65.1 us
  Pallas kernels  62 us (95%)
  local copies, waits for them, and re-layouts  2.23 us (3%)
  between operations  0.81 us (1%)
    pallas_call x1, Pallas kernels, per_device(): pl.pallas_call(kernel, out_shape=outs, in_specs=[any_space] * 5, out_spec...  60.6 us
    unnamed x6, local copies, waits for them, and re-layouts  2.23 us
    pallas_call x1, Pallas kernels, per_device(): pl.pallas_call(store, out_shape=outs, in_specs=[vmem] * 4, out_specs=[any...  1.38 us

profile of v2, /device:TPU:0, one launch (start us, length us, event | category | flops | bytes accessed | tf_op | source)
XLA Modules:
  0.0 65.1 jit_solution(1370982931680165514)
XLA Ops:
  0.6 0.0 copy-start
  0.6 0.7 %copy-done = bf16[32,512]{1,0:T(8,128)(2,1)S(1)} copy-done((bf16[32,512]{1,0:T(8,128)(2,1)S(1)}, bf16[32,512]{1,0:T(8,128)(2,1)}, u32[]{:S(2)}) %copy-start) | copy-done | bytes 32792
  1.4 0.0 copy-start.1
  1.4 0.8 %copy-done.1 = bf16[32,512]{1,0:T(8,128)(2,1)S(1)} copy-done((bf16[32,512]{1,0:T(8,128)(2,1)S(1)}, bf16[32,512]{1,0:T(8,128)(2,1)}, u32[]{:S(2)}) %copy-start.1) | copy-done | bytes 32792
  2.1 0.0 copy-start.2
  2.2 0.7 %copy-done.2 = s32[1024,4]{0,1:T(4,128)S(1)} copy-done((s32[1024,4]{0,1:T(4,128)S(1)}, s32[1024,4]{0,1:T(4,128)}, u32[]{:S(2)}) %copy-start.2) | copy-done | bytes 16408
  2.9 60.6 %shard_map.84 = (f32[512,512]{1,0:T(8,128)S(1)}, f32[512,512]{1,0:T(8,128)S(1)}, f32[32,512]{1,0:T(8,128)S(1)}, f32[32,512]{1,0:T(8,128)S(1)}) custom-call(bf16[2048,512]{1,0:T(8,128)(2,1)} %ent_hbm.1, bf16[2048,512]{1,0:T(8,128)(2,1)} %ett_hbm.1, bf16[32,512]{1,0:T(8,128)(2,1)S(1)} %copy-done, bf16[32,512]{1,0:T(8,128)(2,1)S(1)} %copy-done.1, ...), custom_call_target="tpu_custom_call" | custom-call | tf_op jit(solution)/shard_map/pallas_call | solution.py:407
  63.5 1.4 %shard_map.85 = (f32[512,512]{1,0:T(8,128)}, f32[512,512]{1,0:T(8,128)}, f32[32,512]{1,0:T(8,128)}, f32[32,512]{1,0:T(8,128)}) custom-call(f32[512,512]{1,0:T(8,128)S(1)} %get-tuple-element.8.a, f32[512,512]{1,0:T(8,128)S(1)} %get-tuple-element.9.b, f32[32,512]{1,0:T(8,128)S(1)} %get-tuple-element.10.c, f32[32,512]{1,0:T(8,128)S(1)} %get-tuple-element.11.d), custom_call_target="tpu_custom_call" | custom-call | tf_op jit(solution)/shard_map/pallas_call | solution.py:463
Async XLA Ops:
  0.6 0.8 %copy-start = (bf16[32,512]{1,0:T(8,128)(2,1)S(1)}, bf16[32,512]{1,0:T(8,128)(2,1)}, u32[]{:S(2)}) copy-start(bf16[32,512]{1,0:T(8,128)(2,1)} %q_hbm.1) | copy-start | bytes 98308
  1.4 0.8 %copy-start.1 = (bf16[32,512]{1,0:T(8,128)(2,1)S(1)}, bf16[32,512]{1,0:T(8,128)(2,1)}, u32[]{:S(2)}) copy-start(bf16[32,512]{1,0:T(8,128)(2,1)} %dq_hbm.1) | copy-start | bytes 98308
  2.1 0.7 %copy-start.2 = (s32[1024,4]{0,1:T(4,128)S(1)}, s32[1024,4]{0,1:T(4,128)}, u32[]{:S(2)}) copy-start(s32[1024,4]{0,1:T(4,128)} %param.9) | copy-start | bytes 49156

commit v3 on v2

--- a/solution.py
+++ b/solution.py
@@ -17,7 +17,7 @@
 VMEM_LIMIT = 50 * 2**20
 GNVP, GRAD = 0, 1
 
-A_X, A_Z, A_ZZ, A_XX, A_N = 0, 8, 16, 32, 48
+A_X, A_Z, A_ZZ, A_XX, A_N = 0, 8, 16, 20, 36
 
 
 def dot_nt(a, b):
@@ -182,20 +182,22 @@
     def relays(a):
         for d in (0,) + NEAR_FIRST:
             first_arrived(a, d)
-            j = (4 - d) % 4
-            here = panel[a].at[z, rows(((x + j) % 4) * 32, 32, 32)]
-            for e in NEAR_FIRST:
-                send(here, here, *slot(a, A_ZZ + j * 4 + e), pz(e))
-            here = panel[a].at[(z + j) % 4, rows(128 + x * 32, 32, 32)]
-            for e in NEAR_FIRST:
-                send(here, here, *slot(a, A_XX + j * 4 + e), px(e))
+            if d == 0:
+                relay_x(a, 0)
+        for d in NEAR_FIRST:
+            here = panel[a].at[z, pl.ds(0, 128)]
+            send(here, here, *slot(a, A_ZZ + d), pz(d))
+            relay_x(a, 4 - d)
+
+    def relay_x(a, j):
+        here = panel[a].at[(z + j) % 4, rows(128 + x * 32, 32, 32)]
+        for e in NEAR_FIRST:
+            send(here, here, *slot(a, A_XX + j * 4 + e), px(e))
 
     def plane_arrived(a, j):
         p = (z + j) % 4
         if j:
-            for i in range(4):
-                there = panel[a].at[p, rows(((x + i) % 4) * 32, 32, 32)]
-                arrived(there, *slot(a, A_ZZ + i * 4 + (4 - j)))
+            arrived(panel[a].at[p, pl.ds(0, 128)], *slot(a, A_ZZ + 4 - j))
         for d in NEAR_FIRST:
             there = panel[a].at[p, rows(128 + ((x - d + 4) % 4) * 32, 32, 32)]
             arrived(there, *slot(a, A_XX + j * 4 + d))
@@ -222,39 +224,40 @@
     def add(ref, value, first):
         ref[...] = value if first else ref[...] + value
 
-    def grad_tile(j, far, first):
+    def grad_tile(j, s, n, new, first):
         p = (z + j) % 4
-        half = 1 - yh if far else yh
-        es = rows(half * 2 * SUB, 2 * SUB, 2 * SUB)
+        es = rows(s * SUB, n * SUB, SUB)
         q = qp[p]
         e = ent[es]
         score = dot_nt(q, e)
         lane = lax.broadcasted_iota(I32, (PLANE, 128), 1)
         label = []
-        for b in range(2 * SUB // 128):
-            ids = lane + (half * 2 * SUB + b * 128)
+        for b in range(n * SUB // 128):
+            ids = lane + (s * SUB + b * 128)
             hit = tb[0, p] == ids
             for k in range(1, 4):
                 hit = hit | (tb[k, p] == ids)
             label.append(jnp.where(hit, 1.0, 0.0).astype(F32))
         label = jnp.concatenate(label, axis=1)
         prob = 1.0 / (1.0 + jnp.exp(-score))
-        w[half, p] = prob * (1.0 - prob)
+        slope = prob * (1.0 - prob)
+        for i in range(n):
+            w[p, s + i] = slope[:, i * SUB : (i + 1) * SUB]
         ugrad = (prob - label).astype(BF16)
-        add(qacc.at[GRAD, p], dot_nn(ugrad, e), far)
+        add(qacc.at[GRAD, p], dot_nn(ugrad, e), new)
         add(eacc.at[GRAD, es], dot_tn(ugrad, q), first)
 
-    def gnvp_tile(j, far, first):
+    def gnvp_tile(j, s, n, new, first):
         p = (z + j) % 4
-        half = 1 - yh if far else yh
-        es = rows(half * 2 * SUB, 2 * SUB, 2 * SUB)
+        es = rows(s * SUB, n * SUB, SUB)
         q = qp[p]
         e = ent[es]
         dscore = dot_nt(
             jnp.concatenate([dqp[p], q], axis=1), jnp.concatenate([e, ett[es]], axis=1)
         )
-        uhess = (w[half, p] * dscore).astype(BF16)
-        add(qacc.at[GNVP, p], dot_nn(uhess, e), far)
+        slope = w[p, s] if n == 1 else jnp.concatenate([w[p, s + i] for i in range(n)], axis=1)
+        uhess = (slope * dscore).astype(BF16)
+        add(qacc.at[GNVP, p], dot_nn(uhess, e), new)
         add(eacc.at[GNVP, es], dot_tn(uhess, q), first)
 
     far_other = (1 - yh) * 2 + 1 - c
@@ -315,7 +318,7 @@
         for d in NEAR_FIRST:
             here = b2s.at[k, 0, rows(((x + d) % 4) * 32, 32, 32)]
             send(here, b2r.at[k, d], b2_ss.at[k, d], b2_rs.at[k, d], px(d))
-        for j in (2, 1, 3, 0):
+        for j in (3, 1, 2, 0):
             total = qacc[k, (z + j) % 4, rows(128 + x * 32, 32, 32)]
             for d in NEAR_FIRST:
                 arrived(br1s.at[k, j, d], b1s_ss.at[k, j, d], b1s_rs.at[k, j, d])
@@ -342,41 +345,41 @@
             arrived(b3r.at[k, h], b3_ss.at[k, h], b3_rs.at[k, h])
             out[pl.ds(h * 16, 16)] = b3s[k, h, rows(yl * 16, 16, 16)] + b3r[k, h]
 
-    for j in (0,) + NEAR_FIRST:
+    far, near = (1 - yh) * 2, yh * 2
+    for j in (0, 3, 1):
         plane_arrived(0, j)
-        grad_tile(j, True, j == 0)
+        grad_tile(j, far, 2, True, j == 0)
+    plane_arrived(0, 2)
+    grad_tile(2, far_other, 1, True, False)
     to_core(GRAD, 0, far_other)
-    grad_tile(2, False, True)
-    to_1(GRAD, 2)
-    grad_tile(1, False, False)
-    to_far(GRAD)
-    to_1(GRAD, 1)
-    grad_tile(3, False, False)
-    to_1(GRAD, 3)
-    grad_tile(0, False, False)
+    grad_tile(2, far_same, 1, False, False)
+    local[6].wait()
+    for j in (3, 1, 2):
+        grad_tile(j, near, 2, False, j == 3)
+        if j == 3:
+            to_far(GRAD)
+        to_1(GRAD, j)
+        plane_arrived(1, j)
+        gnvp_tile(j, far, 2, True, j == 3)
+        gnvp_tile(j, near, 2, False, j == 3)
+        to_1(GNVP, j)
+    plane_arrived(1, 0)
+    gnvp_tile(0, far_other, 1, True, False)
+    to_core(GNVP, 0, far_other)
+    gnvp_tile(0, far_same, 1, False, False)
+    grad_tile(0, near, 2, False, False)
+    to_core(GRAD, 1, near_other)
     to_1(GRAD, 0)
-    to_core(GRAD, 1, near_other)
-    local[6].wait()
-    for j in (0,) + NEAR_FIRST:
-        plane_arrived(1, j)
-        gnvp_tile(j, True, j == 0)
-    to_core(GNVP, 0, far_other)
-    gnvp_tile(2, False, True)
-    to_1(GNVP, 2)
-    gnvp_tile(1, False, False)
     to_far(GNVP)
-    to_1(GNVP, 1)
+    gnvp_tile(0, near, 2, False, False)
+    to_core(GNVP, 1, near_other)
+    to_1(GNVP, 0)
     to_2(GRAD)
-    gnvp_tile(3, False, False)
-    to_1(GNVP, 3)
-    gnvp_tile(0, False, False)
-    to_1(GNVP, 0)
-    to_core(GNVP, 1, near_other)
+    to_2(GNVP)
     to_3(GRAD)
-    to_2(GNVP)
-    finish_queries(GRAD, oqg)
     to_3(GNVP)
     finish_entities(GRAD, oeg)
+    finish_queries(GRAD, oqg)
     finish_queries(GNVP, oqh)
     finish_entities(GNVP, oeh)
     for cp in started:
@@ -407,7 +410,7 @@
     results = pl.pallas_call(
         kernel,
         out_shape=outs,
-        in_specs=[any_space] * 5,
+        in_specs=[pl.BlockSpec(memory_space=pltpu.HBM)] * 5,
         out_specs=[vmem] * 4,
         scratch_shapes=[
             pltpu.VMEM((4 * SUB, D), BF16),
@@ -416,7 +419,7 @@
             pltpu.VMEM((4, PLANE, D), BF16),
             pltpu.VMEM((4, 4 * PLANE), I32),
             pltpu.VMEM((4, 4, PLANE, 128), I32),
-            pltpu.VMEM((2, 4, PLANE, 2 * SUB), F32),
+            pltpu.VMEM((4, 4, PLANE, SUB), F32),
             pltpu.VMEM((2, 4, PLANE, D), F32),
             pltpu.VMEM((2, 4 * SUB, D), F32),
             pltpu.VMEM((2, 2, SUB, D), F32),

time: 65.4 us -> 67.7 us (1.035)
  Pallas kernels: 62 us -> 63.7 us
    pallas_call x1, Pallas kernels: 60.6 us -> 62.3 us  [per_device(): pl.pallas_call(kernel, out_shape=outs, in_specs=[pl.BlockSpec(memory_spac...]
where the time goes in v3:
time: 67.7 us; the launch traced here: 66.7 us
  Pallas kernels  63.7 us (94%)
  local copies, waits for them, and re-layouts  2.23 us (3%)
  between operations  0.81 us (1%)
    pallas_call x1, Pallas kernels, per_device(): pl.pallas_call(kernel, out_shape=outs, in_specs=[pl.BlockSpec(memory_spac...  62.3 us
    unnamed x6, local copies, waits for them, and re-layouts  2.23 us
    pallas_call x1, Pallas kernels, per_device(): pl.pallas_call(store, out_shape=outs, in_specs=[vmem] * 4, out_specs=[any...  1.38 us

profile of v3, /device:TPU:0, one launch (start us, length us, event | category | flops | bytes accessed | tf_op | source)
XLA Modules:
  0.0 66.7 jit_solution(15943448676193401977)
XLA Ops:
  0.6 0.0 copy-start
  0.6 0.7 %copy-done = bf16[32,512]{1,0:T(8,128)(2,1)S(1)} copy-done((bf16[32,512]{1,0:T(8,128)(2,1)S(1)}, bf16[32,512]{1,0:T(8,128)(2,1)}, u32[]{:S(2)}) %copy-start) | copy-done | bytes 32792
  1.4 0.0 copy-start.1
  1.4 0.8 %copy-done.1 = bf16[32,512]{1,0:T(8,128)(2,1)S(1)} copy-done((bf16[32,512]{1,0:T(8,128)(2,1)S(1)}, bf16[32,512]{1,0:T(8,128)(2,1)}, u32[]{:S(2)}) %copy-start.1) | copy-done | bytes 32792
  2.1 0.0 copy-start.2
  2.2 0.7 %copy-done.2 = s32[1024,4]{0,1:T(4,128)S(1)} copy-done((s32[1024,4]{0,1:T(4,128)S(1)}, s32[1024,4]{0,1:T(4,128)}, u32[]{:S(2)}) %copy-start.2) | copy-done | bytes 16408
  2.9 62.3 %shard_map.84 = (f32[512,512]{1,0:T(8,128)S(1)}, f32[512,512]{1,0:T(8,128)S(1)}, f32[32,512]{1,0:T(8,128)S(1)}, f32[32,512]{1,0:T(8,128)S(1)}) custom-call(bf16[2048,512]{1,0:T(8,128)(2,1)} %ent_hbm.1, bf16[2048,512]{1,0:T(8,128)(2,1)} %ett_hbm.1, bf16[32,512]{1,0:T(8,128)(2,1)S(1)} %copy-done, bf16[32,512]{1,0:T(8,128)(2,1)S(1)} %copy-done.1, ...), custom_call_target="tpu_custom_call" | custom-call | tf_op jit(solution)/shard_map/pallas_call | solution.py:410
  65.2 1.4 %shard_map.85 = (f32[512,512]{1,0:T(8,128)}, f32[512,512]{1,0:T(8,128)}, f32[32,512]{1,0:T(8,128)}, f32[32,512]{1,0:T(8,128)}) custom-call(f32[512,512]{1,0:T(8,128)S(1)} %get-tuple-element.8.a, f32[512,512]{1,0:T(8,128)S(1)} %get-tuple-element.9.b, f32[32,512]{1,0:T(8,128)S(1)} %get-tuple-element.10.c, f32[32,512]{1,0:T(8,128)S(1)} %get-tuple-element.11.d), custom_call_target="tpu_custom_call" | custom-call | tf_op jit(solution)/shard_map/pallas_call | solution.py:466
Async XLA Ops:
  0.6 0.8 %copy-start = (bf16[32,512]{1,0:T(8,128)(2,1)S(1)}, bf16[32,512]{1,0:T(8,128)(2,1)}, u32[]{:S(2)}) copy-start(bf16[32,512]{1,0:T(8,128)(2,1)} %q_hbm.1) | copy-start | bytes 98308
  1.4 0.8 %copy-start.1 = (bf16[32,512]{1,0:T(8,128)(2,1)S(1)}, bf16[32,512]{1,0:T(8,128)(2,1)}, u32[]{:S(2)}) copy-start(bf16[32,512]{1,0:T(8,128)(2,1)} %dq_hbm.1) | copy-start | bytes 98308
  2.1 0.7 %copy-start.2 = (s32[1024,4]{0,1:T(4,128)S(1)}, s32[1024,4]{0,1:T(4,128)}, u32[]{:S(2)}) copy-start(s32[1024,4]{0,1:T(4,128)} %param.9) | copy-start | bytes 49156

commit v4 on v2

--- a/solution.py
+++ b/solution.py
@@ -201,7 +201,6 @@
             arrived(there, *slot(a, A_XX + j * 4 + d))
 
     first_sends(0)
-    first_sends(1)
 
     local[4].wait()
 
@@ -216,7 +215,7 @@
 
     lax.fori_loop(0, 8, spread, 0)
     relays(0)
-    relays(1)
+    first_sends(1)
     local[5].wait()
 
     def add(ref, value, first):
@@ -346,10 +345,11 @@
         plane_arrived(0, j)
         grad_tile(j, True, j == 0)
     to_core(GRAD, 0, far_other)
+    relays(1)
     grad_tile(2, False, True)
+    to_far(GRAD)
     to_1(GRAD, 2)
     grad_tile(1, False, False)
-    to_far(GRAD)
     to_1(GRAD, 1)
     grad_tile(3, False, False)
     to_1(GRAD, 3)
@@ -407,7 +407,7 @@
     results = pl.pallas_call(
         kernel,
         out_shape=outs,
-        in_specs=[any_space] * 5,
+        in_specs=[pl.BlockSpec(memory_space=pltpu.HBM)] * 5,
         out_specs=[vmem] * 4,
         scratch_shapes=[
             pltpu.VMEM((4 * SUB, D), BF16),
@@ -459,7 +459,7 @@
         compiler_params=pltpu.CompilerParams(
             collective_id=0, has_side_effects=True, vmem_limit_bytes=VMEM_LIMIT
         ),
-    )(ent_emb, ent_tan, qry_emb, qry_tan, tails.T)
+    )(*[pltpu.with_memory_space_constraint(a, pltpu.HBM) for a in (ent_emb, ent_tan, qry_emb, qry_tan, tails.T)])
     return pl.pallas_call(
         store,
         out_shape=outs,

time: 65.4 us -> 63.2 us (0.966)
  local copies, waits for them, and re-layouts: 2.23 us -> 0 us
    unnamed x6 -> x0, local copies, waits for them, and re-layouts: 2.23 us -> none
where the time goes in v4:
time: 63.2 us; the launch traced here: 63.1 us
  Pallas kernels  62.3 us (99%)
  between operations  0.8 us (1%)
    pallas_call x1, Pallas kernels, per_device(): pl.pallas_call(kernel, out_shape=outs, in_specs=[pl.BlockSpec(memory_spac...  60.9 us
    pallas_call x1, Pallas kernels, per_device(): pl.pallas_call(store, out_shape=outs, in_specs=[vmem] * 4, out_specs=[any...  1.38 us

profile of v4, /device:TPU:0, one launch (start us, length us, event | category | flops | bytes accessed | tf_op | source)
XLA Modules:
  0.0 63.1 jit_solution(15290103865639173957)
XLA Ops:
  0.6 60.9 %shard_map.84 = (f32[512,512]{1,0:T(8,128)S(1)}, f32[512,512]{1,0:T(8,128)S(1)}, f32[32,512]{1,0:T(8,128)S(1)}, f32[32,512]{1,0:T(8,128)S(1)}) custom-call(bf16[2048,512]{1,0:T(8,128)(2,1)} %ent_hbm.1, bf16[2048,512]{1,0:T(8,128)(2,1)} %ett_hbm.1, bf16[32,512]{1,0:T(8,128)(2,1)} %q_hbm.1, bf16[32,512]{1,0:T(8,128)(2,1)} %dq_hbm.1, s32[4,1024]{1,0:T(4,128)} %bitcast.1), custom_call_target="tpu_custom_call" | custom-call | tf_op jit(solution)/shard_map/pallas_call | solution.py:407
  61.5 1.4 %shard_map.85 = (f32[512,512]{1,0:T(8,128)}, f32[512,512]{1,0:T(8,128)}, f32[32,512]{1,0:T(8,128)}, f32[32,512]{1,0:T(8,128)}) custom-call(f32[512,512]{1,0:T(8,128)S(1)} %get-tuple-element.8.a, f32[512,512]{1,0:T(8,128)S(1)} %get-tuple-element.9.b, f32[32,512]{1,0:T(8,128)S(1)} %get-tuple-element.10.c, f32[32,512]{1,0:T(8,128)S(1)} %get-tuple-element.11.d), custom_call_target="tpu_custom_call" | custom-call | tf_op jit(solution)/shard_map/pallas_call | solution.py:463

commit v5 on v4

--- a/solution.py
+++ b/solution.py
@@ -74,7 +74,10 @@
     br1,
     br1s,
     b2s,
+    b2q,
+    b2qs,
     b2r,
+    b2rs,
     b3s,
     b3r,
     lsem,
@@ -96,6 +99,8 @@
     b1s_rs,
     b2_ss,
     b2_rs,
+    b2s_ss,
+    b2s_rs,
     b3_ss,
     b3_rs,
 ):
@@ -311,8 +316,10 @@
             arrived(br0.at[k, j], b0_ss.at[k, j], b0_rs.at[k, j])
             total = total + dequantize(br0.at[k, j], br0s.at[k, j])
         b2s[k, 0] = total
+        quantize(total, b2q.at[k, 0], b2qs.at[k, 0])
         for d in NEAR_FIRST:
-            here = b2s.at[k, 0, rows(((x + d) % 4) * 32, 32, 32)]
+            send(b2qs.at[k, 0], b2rs.at[k, d], b2s_ss.at[k, d], b2s_rs.at[k, d], px(d))
+            here = b2q.at[k, 0, rows(((x + d) % 4) * 32, 32, 32)]
             send(here, b2r.at[k, d], b2_ss.at[k, d], b2_rs.at[k, d], px(d))
         for j in (2, 1, 3, 0):
             total = qacc[k, (z + j) % 4, rows(128 + x * 32, 32, 32)]
@@ -321,17 +328,21 @@
                 arrived(br1.at[k, j, d], b1_ss.at[k, j, d], b1_rs.at[k, j, d])
                 total = total + dequantize(br1.at[k, j, d], br1s.at[k, j, d])
             b2s[k, 1, pl.ds(j * 32, 32)] = total
-            if j:
-                here = b2s.at[k, 1, pl.ds(j * 32, 32)]
-                send(here, b2r.at[k, 4 + j], b2_ss.at[k, 4 + j], b2_rs.at[k, 4 + j], pz(j))
+        quantize(b2s[k, 1], b2q.at[k, 1], b2qs.at[k, 1])
+        for j in NEAR_FIRST:
+            i = 4 + j
+            send(b2qs.at[k, 1], b2rs.at[k, i], b2s_ss.at[k, i], b2s_rs.at[k, i], pz(j))
+            here = b2q.at[k, 1, pl.ds(j * 32, 32)]
+            send(here, b2r.at[k, i], b2_ss.at[k, i], b2_rs.at[k, i], pz(j))
 
     def to_3(k):
         for h in (0, 1):
             total = b2s[k, 0, rows(x * 32, 32, 32)] if h == 0 else b2s[k, 1, pl.ds(0, 32)]
             for d in NEAR_FIRST:
                 i = h * 4 + d
+                arrived(b2rs.at[k, i], b2s_ss.at[k, i], b2s_rs.at[k, i])
                 arrived(b2r.at[k, i], b2_ss.at[k, i], b2_rs.at[k, i])
-                total = total + b2r[k, i]
+                total = total + dequantize(b2r.at[k, i], b2rs.at[k, i])
             b3s[k, h] = total
             here = b3s.at[k, h, rows((1 - yl) * 16, 16, 16)]
             send(here, b3r.at[k, h], b3_ss.at[k, h], b3_rs.at[k, h], py)
@@ -363,8 +374,8 @@
     to_core(GNVP, 0, far_other)
     gnvp_tile(2, False, True)
     to_1(GNVP, 2)
+    to_far(GNVP)
     gnvp_tile(1, False, False)
-    to_far(GNVP)
     to_1(GNVP, 1)
     to_2(GRAD)
     gnvp_tile(3, False, False)
@@ -431,7 +442,10 @@
             pltpu.VMEM((2, 4, 4, 32, D), I16),
             pltpu.VMEM((2, 4, 4, 8, 128), F32),
             pltpu.VMEM((2, 2, 128, D), F32),
-            pltpu.VMEM((2, 8, 32, D), F32),
+            pltpu.VMEM((2, 2, 128, D), I16),
+            pltpu.VMEM((2, 2, 8, 128), F32),
+            pltpu.VMEM((2, 8, 32, D), I16),
+            pltpu.VMEM((2, 8, 8, 128), F32),
             pltpu.VMEM((2, 2, 32, D), F32),
             pltpu.VMEM((2, 2, 16, D), F32),
             dma((7,)),
@@ -453,6 +467,8 @@
             dma((2, 4, 4)),
             dma((2, 8)),
             dma((2, 8)),
+            dma((2, 8)),
+            dma((2, 8)),
             dma((2, 2)),
             dma((2, 2)),
         ],

time: 63.2 us -> 62.5 us (0.989)
  Pallas kernels: 62.3 us -> 61.5 us
    pallas_call x1, Pallas kernels: 60.9 us -> 60.1 us  [per_device(): pl.pallas_call(kernel, out_shape=outs, in_specs=[pl.BlockSpec(memory_spac...]
where the time goes in v5:
time: 62.5 us; the launch traced here: 62.3 us
  Pallas kernels  61.5 us (98%)
  between operations  0.8 us (1%)
    pallas_call x1, Pallas kernels, per_device(): pl.pallas_call(kernel, out_shape=outs, in_specs=[pl.BlockSpec(memory_spac...  60.1 us
    pallas_call x1, Pallas kernels, per_device(): pl.pallas_call(store, out_shape=outs, in_specs=[vmem] * 4, out_specs=[any...  1.38 us

profile of v5, /device:TPU:0, one launch (start us, length us, event | category | flops | bytes accessed | tf_op | source)
XLA Modules:
  0.0 62.3 jit_solution(11596500452124204948)
XLA Ops:
  0.6 60.1 %shard_map.84 = (f32[512,512]{1,0:T(8,128)S(1)}, f32[512,512]{1,0:T(8,128)S(1)}, f32[32,512]{1,0:T(8,128)S(1)}, f32[32,512]{1,0:T(8,128)S(1)}) custom-call(bf16[2048,512]{1,0:T(8,128)(2,1)} %ent_hbm.1, bf16[2048,512]{1,0:T(8,128)(2,1)} %ett_hbm.1, bf16[32,512]{1,0:T(8,128)(2,1)} %q_hbm.1, bf16[32,512]{1,0:T(8,128)(2,1)} %dq_hbm.1, s32[4,1024]{1,0:T(4,128)} %bitcast.1), custom_call_target="tpu_custom_call" | custom-call | tf_op jit(solution)/shard_map/pallas_call | solution.py:418
  60.8 1.4 %shard_map.85 = (f32[512,512]{1,0:T(8,128)}, f32[512,512]{1,0:T(8,128)}, f32[32,512]{1,0:T(8,128)}, f32[32,512]{1,0:T(8,128)}) custom-call(f32[512,512]{1,0:T(8,128)S(1)} %get-tuple-element.8.a, f32[512,512]{1,0:T(8,128)S(1)} %get-tuple-element.9.b, f32[32,512]{1,0:T(8,128)S(1)} %get-tuple-element.10.c, f32[32,512]{1,0:T(8,128)S(1)} %get-tuple-element.11.d), custom_call_target="tpu_custom_call" | custom-call | tf_op jit(solution)/shard_map/pallas_call | solution.py:479
